TPU v7x, 32 devices: a whole 2x2x4 slice. The times are simulated.
32 devices in a mesh: view: 8 (over z, core), span: 4 (over y, x).
Axes of the slice: x: 2, y: 2, z: 4, core: 2. Of those that a mesh axis runs over, the one named last changes fastest.
Arguments:
- tokens: bfloat16 [8, 1024, 1024], P('view', 'span'), may hold values from -6 to 6
- scan_order: int32 [8, 1024], P('view'), may hold values from 0 to 1023, as said below
- w_merge: bfloat16 [4096, 1024], replicated, may hold values from -0.09375 to 0.09375
- bias: bfloat16 [1024], replicated, may hold values from -4 to 4
- cotangent: bfloat16 [8, 256, 1024], P('view', 'span'), may hold values from -6 to 6
Outputs:
- merged_out: bfloat16 [8, 256, 1024], P('view', 'span')
- token_grad: bfloat16 [8, 1024, 1024], P('view', 'span')
- weight_grad: float32 [4096, 1024], P(('view', 'span'))
- bias_grad: float32 [1024], replicated
Inputs may be any that keep to these rules, and one draw needn't show every extreme that they name: `scan_order`: each row is a permutation of the raster indices of one view. Call tokens 256 * b to 256 * (b + 1) - 1 band b, and scan positions 256 * c to 256 * (c + 1) - 1 block c: every block holds at most 96 tokens of any band, and in every row each block holds exactly 96 tokens of some band.
All inputs are finite; a program needn't handle non-finite values.
Results may differ from a plain program's by a relative error of at most 0.001.
Values may be sent and summed in bfloat16 or wider, within the bound.
No kernel may reach another device: no remote copies, remote signals or barrier semaphores. Data moves between devices by JAX's collectives and lax.ppermute only.
A program may use at most 128 MiB of HBM per device.

v0:
```python
import math
import jax
import jax.numpy as jnp
from jax import lax
from jax.sharding import PartitionSpec as P

COLS = 128


def body(tokens, scan_order, w_merge, bias, cotangent):
    spans = lax.axis_size("span")
    views = lax.axis_size("view")
    span_index = lax.axis_index("span")
    tok_dev = tokens.shape[1]
    width = tokens.shape[2]
    capacity = 3 * (tok_dev // spans) // 2
    rows_dev = tok_dev // COLS
    order_all = scan_order[0].reshape(spans, tok_dev)
    owners = order_all // tok_dev
    owner_hot = (owners[:, :, None] == jnp.arange(spans, dtype=jnp.int32)[None, None, :]).astype(
        jnp.int32
    )
    slot_rank = jnp.sum((jnp.cumsum(owner_hot, axis=1) - 1) * owner_hot, axis=2)
    dest_slots = owners * capacity + slot_rank
    my_slots = lax.dynamic_index_in_dim(dest_slots, span_index, 0, keepdims=False)
    outgoing = jnp.zeros((spans * capacity, width), jnp.bfloat16).at[my_slots].set(tokens[0])
    received = lax.all_to_all(
        outgoing.reshape(spans, capacity, width), "span", split_axis=0, concat_axis=0, tiled=True
    )
    arriving = owners == span_index
    source_slot = jnp.arange(spans, dtype=jnp.int32)[:, None] * capacity + slot_rank
    local_index = jnp.where(arriving, order_all - span_index * tok_dev, tok_dev)
    source_of = (
        jnp.zeros((tok_dev,), jnp.int32)
        .at[local_index.reshape(-1)]
        .set(source_slot.reshape(-1), mode="drop")
    )
    raster = received.reshape(spans * capacity, width)[source_of]
    merged = (
        raster.reshape(rows_dev // 2, 2, COLS // 2, 2, width)
        .transpose(0, 2, 1, 3, 4)
        .reshape(tok_dev // 4, 4 * width)
    )
    merged_out = (
        jnp.dot(merged, w_merge, preferred_element_type=jnp.float32) + bias.astype(jnp.float32)
    ).astype(jnp.bfloat16)
    grads = cotangent[0]
    grad_merged = lax.dot_general(
        grads, w_merge, (((1,), (1,)), ((), ())), preferred_element_type=jnp.float32
    ).astype(jnp.bfloat16)
    grad_raster = (
        grad_merged.reshape(rows_dev // 2, COLS // 2, 2, 2, width)
        .transpose(0, 2, 1, 3, 4)
        .reshape(tok_dev, width)
    )
    going_back = jnp.zeros((spans * capacity, width), jnp.bfloat16).at[source_of].set(grad_raster)
    returned = lax.all_to_all(
        going_back.reshape(spans, capacity, width), "span", split_axis=0, concat_axis=0, tiled=True
    )
    token_grad = returned.reshape(spans * capacity, width)[my_slots]
    kernel_rows = 4 * width
    merged_rows = merged.shape[0]
    group_rows = kernel_rows // (views * spans)
    regrouped = merged.reshape(merged_rows, views, spans, group_rows).transpose(0, 2, 1, 3)
    view_tokens = lax.all_to_all(regrouped, "span", split_axis=1, concat_axis=0, tiled=True)
    view_tokens = view_tokens.reshape(spans * merged_rows, views * group_rows)
    all_grads = lax.all_gather(grads, "span", axis=0, tiled=True)
    partial_sum = lax.dot_general(
        view_tokens, all_grads, (((0,), (0,)), ((), ())), preferred_element_type=jnp.float32
    )
    weight_sum = lax.psum_scatter(partial_sum, "view", scatter_dimension=0, tiled=True)
    bias_total = lax.psum(jnp.sum(grads.astype(jnp.float32), axis=0), ("view", "span"))
    grad_scale = 1.0 / math.sqrt(views * spans * (tok_dev // 4))
    return (merged_out[None], token_grad[None], weight_sum * grad_scale, bias_total * grad_scale)


def solution(mesh):
    in_specs = (P("view", "span", None), P("view", None), P(), P(), P("view", "span", None))
    out_specs = (P("view", "span", None), P("view", "span", None), P(("view", "span"), None), P())
    return jax.shard_map(body, mesh=mesh, in_specs=in_specs, out_specs=out_specs, check_vma=False)
```

profile of v0, /device:TPU:0, one launch (start us, length us, event | category | flops | bytes accessed | tf_op | source)
XLA Modules:
  0.0 131.2 jit_solution(6496516762859729099)
XLA Ops:
  7.2 0.0 copy-start
  7.2 0.0 copy-start.1
  7.2 0.8 and_select_fusion.1
  8.0 4.8 %reduce-window.6 = s32[4,4,2,128]{3,2,1,0:T(2,128)S(1)} reduce-window(s32[4,4,2,128]{3,2,1,0:T(2,128)S(1)} %compare_convert_fusion, s32[]{:T(128)} %constant.19.clone.1), window={size=1x1x1x128 pad=0_0x0_0x0_0x127_0}, to_apply=%region_0.1 | reduce-window | flops 520192 | bytes 32772 | tf_op jit(solution)/shard_map/reduce-window
  12.8 0.1 slice.12
  12.9 0.1 copy.16
  13.0 0.1 copy.17
  13.2 0.1 add_add_fusion
  13.3 0.5 broadcast.237
  13.8 1.3 %reduce.3 = s32[1024]{0:T(1024)S(1)} reduce(s32[1,1024]{1,0:T(1,128)} %param.6, s32[]{:T(128)} %broadcast.237), dimensions={0}, to_apply=%param.6.reduce_sub_computation.3 | reduce | bytes 8196 | tf_op args[1]
  15.2 0.0 copy-done
  15.2 2.6 %scatter_custom_fusion = bf16[384,1024]{1,0:T(8,128)(2,1)} fusion(s32[256]{0:T(256)S(1)} %bitcast.75, bf16[1,256,1024]{2,1,0:T(8,128)(2,1)S(1)} %copy-done, bf16[]{:T(256)} %constant.15.clone.1), kind=kCustom, calls=%fused_computation.13 | custom fusion | bytes 1310722 | tf_op jit(solution)/shard_map/scatter | solution.py:26
  17.8 5.2 %all-to-all-start = ((bf16[4,96,1024]{2,1,0:T(8,128)(2,1)}), bf16[4,96,1024]{2,1,0:T(8,128)(2,1)S(1)}, u32[]{:S(2)}, u32[]{:S(2)}) async-start(bf16[4,96,1024]{2,1,0:T(8,128)(2,1)} %bitcast.6), calls=%async_computation | async-start | bytes 1572864 | tf_op jit(solution)/shard_map/all_to_all | solution.py:27
  23.0 0.1 add_bitcast_fusion
  23.1 0.7 compare_select_fusion
  23.8 4.3 %scatter_custom_fusion.1 = s32[256]{0:T(256)S(1)} fusion(s32[1024]{0:T(1024)S(1)} %bitcast.78, s32[1024]{0:T(1024)S(1)} %bitcast.77, s32[]{:T(128)} %constant.19.clone.1), kind=kCustom, calls=%fused_computation.59 | custom fusion | bytes 1028 | tf_op jit(solution)/shard_map/scatter | solution.py:36
  28.2 5.7 %all-to-all-done = bf16[4,96,1024]{2,1,0:T(8,128)(2,1)S(1)} async-done(((bf16[4,96,1024]{2,1,0:T(8,128)(2,1)}), bf16[4,96,1024]{2,1,0:T(8,128)(2,1)S(1)}, u32[]{:S(2)}, u32[]{:S(2)}) %all-to-all-start) | async-done | bytes 786464 | tf_op jit(solution)/shard_map/all_to_all | solution.py:27
  33.8 1.2 gather_fusion
  35.0 0.2 reshape.224
  35.2 0.4 copy.30
  35.6 0.3 reshape_reshape.3
  35.9 0.9 copy.20
  36.8 3.5 %all-to-all-start.2 = ((bf16[64,4,8,128]{3,2,0,1:T(8,128)(2,1)}), bf16[64,4,8,128]{3,2,0,1:T(8,128)(2,1)S(1)}, u32[]{:S(2)}, u32[]{:S(2)}) async-start(bf16[64,4,8,128]{3,2,0,1:T(8,128)(2,1)} %copy.20), calls=%async_computation.2 | async-start | bytes 1048576 | tf_op jit(solution)/shard_map/all_to_all | solution.py:65
  40.3 0.0 reduce-scatter.2.cloned.1.call-start
  40.3 0.0 copy-done.1
  40.3 13.7 %all-gather = bf16[1,256,1024]{2,1,0:T(8,128)(2,1)S(1)} all-gather(bf16[1,64,1024]{2,1,0:T(8,128)(2,1)S(1)} %copy-done.1), channel_id=2, replica_groups=mesh['view'=8,'span'=4] {'span'}, dimensions={1}, use_global_device_ids=true | all-gather | bytes 655360 | tf_op jit(solution)/shard_map/all_gather | solution.py:67
  54.0 0.0 all-to-all-done.2
  54.0 2.7 %fusion.2 = f32[1024,1024]{1,0:T(8,128)} fusion(bf16[32,8,8,128]{3,2,1,0:T(8,128)(2,1)S(1)} %bitcast.70, bf16[1,256,1024]{2,1,0:T(8,128)(2,1)S(1)} %all-gather), kind=kOutput, calls=%fused_computation.9 | convolution fusion | flops 536870912 | bytes 5242880 | tf_op jit(solution)/shard_map/dot_general | solution.py:68
  56.7 0.0 copy-start.2
  56.7 0.0 reduce-scatter.2.cloned.1.call-update
  56.7 6.0 %convolution_convert_fusion = bf16[64,4096]{1,0:T(8,128)(2,1)S(1)} fusion(bf16[4096,1024]{1,0:T(8,128)(2,1)} %param.7, bf16[1,64,1024]{2,1,0:T(8,128)(2,1)S(1)} %copy-done.1), kind=kOutput, calls=%fused_computation.5 | convolution fusion | flops 537133056 | bytes 9043968 | tf_op jit(solution)/shard_map/dot_general | solution.py:48
  62.8 0.4 reshape.226
  63.1 0.4 copy.29
  63.5 0.2 reshape.267
  63.7 2.6 %scatter_custom_fusion.2 = bf16[384,1024]{1,0:T(8,128)(2,1)} fusion(s32[256]{0:T(256)S(1)} %compare_select_fusion.6, bf16[256,1024]{1,0:T(8,128)(2,1)S(1)} %reshape.267, bf16[]{:T(256)} %constant.15.clone.1), kind=kCustom, calls=%fused_computation.17 | custom fusion | bytes 786434 | tf_op jit(solution)/shard_map/scatter | solution.py:56
  66.3 3.5 %all-to-all-start.1 = ((bf16[4,96,1024]{2,1,0:T(8,128)(2,1)}), bf16[4,96,1024]{2,1,0:T(8,128)(2,1)S(1)}, u32[]{:S(2)}, u32[]{:S(2)}) async-start(bf16[4,96,1024]{2,1,0:T(8,128)(2,1)} %bitcast.14), calls=%async_computation.1 | async-start | bytes 1572864 | tf_op jit(solution)/shard_map/all_to_all | solution.py:57
  69.8 0.0 copy-done.2
  69.9 44.0 %psum.7 = f32[1024]{0:T(1024)S(1)} all-reduce(f32[1024]{0:T(1024)S(1)} %convert_reduce_fusion), channel_id=1, replica_groups=mesh['view'=8,'span'=4] {'view','span'}, use_global_device_ids=true, to_apply=%region_8.9 | all-reduce | flops 1024 | bytes 8192 | tf_op jit(solution)/shard_map/psum | solution.py:72
  113.8 0.6 broadcast_multiply_fusion.1
  114.4 0.4 reshape.225
  114.8 0.0 all-to-all-done.1
  114.8 2.0 %gather_fusion.1 = bf16[256,1024]{1,0:T(8,128)(2,1)} fusion(bf16[384,1024]{1,0:T(8,128)(2,1)S(1)} %bitcast.67, s32[1024]{0:T(1024)S(1)} %pad_clamp_fusion), kind=kCustom, calls=%fused_computation.1 | custom fusion | bytes 1049600 | tf_op jit(solution)/shard_map/gather | solution.py:60
  116.8 5.6 %fusion.1 = bf16[1,64,1024]{2,1,0:T(8,128)(2,1)} fusion(bf16[64,4096]{1,0:T(8,128)(2,1)S(1)} %reshape.225, bf16[4096,1024]{1,0:T(8,128)(2,1)} %param.7, f32[1024]{0:T(1024)S(1)} %convert_element_type.18), kind=kOutput, calls=%fused_computation.8 | convolution fusion | flops 537001984 | bytes 9048064 | tf_op jit(solution)/shard_map/dot_general | solution.py:45
  122.4 0.0 reduce-scatter.2.cloned.1.call-done
  122.4 1.9 %broadcast_multiply_fusion = f32[128,1024]{1,0:T(8,128)} fusion(f32[128,1024]{1,0:T(8,128)} %reduce-scatter.2.cloned.1.call-done), kind=kLoop, calls=%fused_computation.21 | loop fusion | flops 131072 | bytes 1048576 | tf_op jit(solution)/shard_map/mul | solution.py:74
  (15 shorter events, 0.2 us)
Async XLA Ops:
  7.2 8.1 %copy-start = (bf16[1,256,1024]{2,1,0:T(8,128)(2,1)S(1)}, bf16[1,256,1024]{2,1,0:T(8,128)(2,1)}, u32[]{:S(2)}) copy-start(bf16[1,256,1024]{2,1,0:T(8,128)(2,1)} %param.5) | copy-start | bytes 1572868
  7.2 33.1 %copy-start.1 = (bf16[1,64,1024]{2,1,0:T(8,128)(2,1)S(1)}, bf16[1,64,1024]{2,1,0:T(8,128)(2,1)}, u32[]{:S(2)}) copy-start(bf16[1,64,1024]{2,1,0:T(8,128)(2,1)} %param.9) | copy-start | bytes 393220
  17.8 16.0 %all-to-all-start = ((bf16[4,96,1024]{2,1,0:T(8,128)(2,1)}), bf16[4,96,1024]{2,1,0:T(8,128)(2,1)S(1)}, u32[]{:S(2)}, u32[]{:S(2)}) async-start(bf16[4,96,1024]{2,1,0:T(8,128)(2,1)} %bitcast.6), calls=%async_computation | async-start | bytes 1572864 | tf_op jit(solution)/shard_map/all_to_all | solution.py:27
  36.8 17.2 %all-to-all-start.2 = ((bf16[64,4,8,128]{3,2,0,1:T(8,128)(2,1)}), bf16[64,4,8,128]{3,2,0,1:T(8,128)(2,1)S(1)}, u32[]{:S(2)}, u32[]{:S(2)}) async-start(bf16[64,4,8,128]{3,2,0,1:T(8,128)(2,1)} %copy.20), calls=%async_computation.2 | async-start | bytes 1048576 | tf_op jit(solution)/shard_map/all_to_all | solution.py:65
  40.3 82.2 %reduce-scatter.2.cloned.1.call-start = ((), (), s32[]{:S(2)}) async-start(), calls=%async_computation.4 | async-start | bytes 4718592 | tf_op jit(solution)/shard_map/reduce_scatter | solution.py:71
  56.7 13.1 %copy-start.2 = (bf16[1024]{0:T(1024)(128)(2,1)S(1)}, bf16[1024]{0:T(1024)(128)(2,1)}, u32[]{:S(2)}) copy-start(bf16[1024]{0:T(1024)(128)(2,1)} %param.8) | copy-start | bytes 6148
  66.3 48.5 %all-to-all-start.1 = ((bf16[4,96,1024]{2,1,0:T(8,128)(2,1)}), bf16[4,96,1024]{2,1,0:T(8,128)(2,1)S(1)}, u32[]{:S(2)}, u32[]{:S(2)}) async-start(bf16[4,96,1024]{2,1,0:T(8,128)(2,1)} %bitcast.14), calls=%async_computation.1 | async-start | bytes 1572864 | tf_op jit(solution)/shard_map/all_to_all | solution.py:57
Sparse Core Ops, SparseCore 0:
  56.8 51.2 reduce-scatter.1
where the time goes:
time: 132 us; the launch traced here: 131 us
  blocking collectives  57.6 us (44%)
  local copies, waits for them, and re-layouts  16.6 us (13%)
  matrix products  14.3 us (11%)
  between operations  14.2 us (11%)
  starting transfers between devices  12.2 us (9%)
  other arithmetic  10.4 us (8%)
  waiting for transfers between devices  5.71 us (4%)
    psum x1, blocking collectives, body(): lax.psum(jnp.sum(grads.astype(jnp.float32), axis=0), ('view', 'span'))  44 us
    all_gather x1, blocking collectives, body(): all_grads = lax.all_gather(grads, 'span', axis=0, tiled=True)  13.7 us
    dot_general x1, matrix products, body(): lax.dot_general(grads, w_merge, (((1,), (1,)), ((), ())), preferred_eleme...  6.04 us
    all_to_all x1, waiting for transfers between devices, body(): lax.all_to_all(outgoing.reshape(spans, capacity, width), 'span', split_ax...  5.69 us
    dot_general x1, matrix products, body(): jnp.dot(merged, w_merge, preferred_element_type=jnp.float32)  5.61 us
    all_to_all x1, starting transfers between devices, body(): lax.all_to_all(outgoing.reshape(spans, capacity, width), 'span', split_ax...  5.19 us
    another operation x2, other arithmetic  4.84 us
    scatter x1, local copies, waits for them, and re-layouts, body(): source_of = jnp.zeros((tok_dev,), jnp.int32).at[local_index.reshape(-1)]....  4.3 us
  transfers between devices with their start and end apart: 4, of which 1 were waited for; matrix products, arithmetic and copies ran while one was open for 18% of the time, Pallas kernels for 0%

commit v1 on v0

--- a/solution.py
+++ b/solution.py
@@ -64,7 +64,14 @@
     regrouped = merged.reshape(merged_rows, views, spans, group_rows).transpose(0, 2, 1, 3)
     view_tokens = lax.all_to_all(regrouped, "span", split_axis=1, concat_axis=0, tiled=True)
     view_tokens = view_tokens.reshape(spans * merged_rows, views * group_rows)
-    all_grads = lax.all_gather(grads, "span", axis=0, tiled=True)
+    ways, here = (lax.axis_size("span"), lax.axis_index("span"))
+    all_grads, reach = (grads, 1)
+    while reach < ways:
+        theirs = lax.ppermute(all_grads, "span", [(d, d ^ reach) for d in range(ways)])
+        mine_first = jnp.concatenate([all_grads, theirs], axis=0)
+        theirs_first = jnp.concatenate([theirs, all_grads], axis=0)
+        all_grads = jnp.where(here & reach == 0, mine_first, theirs_first)
+        reach = 2 * reach
     partial_sum = lax.dot_general(
         view_tokens, all_grads, (((0,), (0,)), ((), ())), preferred_element_type=jnp.float32
     )

time: 132 us -> 132 us (level)
  blocking collectives: 57.6 us -> 45 us
  waiting for transfers between devices: 5.71 us -> 14.6 us
  starting transfers between devices: 12.2 us -> 16.2 us
    all_gather x1 -> x0, blocking collectives: 13.7 us -> none  [body(): all_grads = lax.all_gather(grads, 'span', axis=0, tiled=True)]
    ppermute x0 -> x2, waiting for transfers between devices: none -> 9.59 us  [body(): lax.ppermute(all_grads, 'span', [(d, d ^ reach) for d in range(ways)])]
    ppermute x0 -> x2, starting transfers between devices: none -> 4.01 us  [body(): lax.ppermute(all_grads, 'span', [(d, d ^ reach) for d in range(ways)])]
  transfers between devices with their start and end apart: 4 -> 6, of which waited for: 1 -> 2; matrix products, arithmetic and copies ran while one was open for 18% -> 20% of each run, Pallas kernels for 0% -> 0%
where the time goes in v1:
time: 132 us
  blocking collectives  45 us (34%)
  local copies, waits for them, and re-layouts  16.6 us (13%)
  starting transfers between devices  16.2 us (12%)
  waiting for transfers between devices  14.6 us (11%)
  matrix products  14.3 us (11%)
  between operations  14.3 us (11%)
  other arithmetic  10.5 us (8%)
    psum x1, blocking collectives, body(): lax.psum(jnp.sum(grads.astype(jnp.float32), axis=0), ('view', 'span'))  45 us
    ppermute x2, waiting for transfers between devices, body(): lax.ppermute(all_grads, 'span', [(d, d ^ reach) for d in range(ways)])  9.59 us
    dot_general x1, matrix products, body(): lax.dot_general(grads, w_merge, (((1,), (1,)), ((), ())), preferred_eleme...  6.04 us
    dot_general x1, matrix products, body(): jnp.dot(merged, w_merge, preferred_element_type=jnp.float32)  5.61 us
    all_to_all x1, starting transfers between devices, body(): lax.all_to_all(outgoing.reshape(spans, capacity, width), 'span', split_ax...  5.19 us
    all_to_all x1, waiting for transfers between devices, body(): lax.all_to_all(outgoing.reshape(spans, capacity, width), 'span', split_ax...  5.03 us
    another operation x2, other arithmetic  4.84 us
    scatter x1, local copies, waits for them, and re-layouts, body(): source_of = jnp.zeros((tok_dev,), jnp.int32).at[local_index.reshape(-1)]....  4.3 us
  transfers between devices with their start and end apart: 6, of which 2 were waited for; matrix products, arithmetic and copies ran while one was open for 20% of the time, Pallas kernels for 0%

profile of v1, /device:TPU:0, one launch (start us, length us, event | category | flops | bytes accessed | tf_op | source)
XLA Modules:
  0.0 131.5 jit_solution(13441503164099892250)
XLA Ops:
  7.2 0.0 copy-start
  7.2 0.0 copy-start.1
  7.2 0.8 and_select_fusion.1
  8.0 4.8 %reduce-window.6 = s32[4,4,2,128]{3,2,1,0:T(2,128)S(1)} reduce-window(s32[4,4,2,128]{3,2,1,0:T(2,128)S(1)} %compare_convert_fusion, s32[]{:T(128)} %constant.17.clone.1), window={size=1x1x1x128 pad=0_0x0_0x0_0x127_0}, to_apply=%region_0.1 | reduce-window | flops 520192 | bytes 32772 | tf_op jit(solution)/shard_map/reduce-window
  12.8 0.1 slice.12
  12.9 0.1 copy.16
  13.0 0.1 copy.17
  13.2 0.1 add_add_fusion
  13.3 0.5 broadcast.237
  13.8 1.3 %reduce.3 = s32[1024]{0:T(1024)S(1)} reduce(s32[1,1024]{1,0:T(1,128)} %param.6, s32[]{:T(128)} %broadcast.237), dimensions={0}, to_apply=%param.6.reduce_sub_computation.3 | reduce | bytes 8196 | tf_op args[1]
  15.2 0.0 copy-done
  15.2 2.6 %scatter_custom_fusion = bf16[384,1024]{1,0:T(8,128)(2,1)} fusion(s32[256]{0:T(256)S(1)} %bitcast.74, bf16[1,256,1024]{2,1,0:T(8,128)(2,1)S(1)} %copy-done, bf16[]{:T(256)} %constant.15.clone.1), kind=kCustom, calls=%fused_computation.18 | custom fusion | bytes 1310722 | tf_op jit(solution)/shard_map/scatter | solution.py:26
  17.8 5.2 %all-to-all-start = ((bf16[4,96,1024]{2,1,0:T(8,128)(2,1)}), bf16[4,96,1024]{2,1,0:T(8,128)(2,1)S(1)}, u32[]{:S(2)}, u32[]{:S(2)}) async-start(bf16[4,96,1024]{2,1,0:T(8,128)(2,1)} %bitcast.6), calls=%async_computation | async-start | bytes 1572864 | tf_op jit(solution)/shard_map/all_to_all | solution.py:27
  23.0 2.0 %collective-permute-start = (bf16[64,1024]{1,0:T(8,128)(2,1)}, bf16[64,1024]{1,0:T(8,128)(2,1)S(1)}, u32[]{:S(2)}, u32[]{:S(2)}) collective-permute-start(bf16[64,1024]{1,0:T(8,128)(2,1)} %bitcast.70), channel_id=1, source_target_pairs={{0,1},{1,0},{2,3},{3,2},{4,5},{5,4},{6,7},{7,6},{8,9},{9,8},{10,11... | collective-permute-start | bytes 393224 | tf_op jit(solution)/shard_map/ppermute | solution.py:70
  25.0 0.1 add_bitcast_fusion
  25.1 0.7 compare_select_fusion
  25.8 4.3 %scatter_custom_fusion.1 = s32[256]{0:T(256)S(1)} fusion(s32[1024]{0:T(1024)S(1)} %bitcast.77, s32[1024]{0:T(1024)S(1)} %bitcast.76, s32[]{:T(128)} %constant.17.clone.1), kind=kCustom, calls=%fused_computation.65 | custom fusion | bytes 1028 | tf_op jit(solution)/shard_map/scatter | solution.py:36
  30.2 5.0 %all-to-all-done = bf16[4,96,1024]{2,1,0:T(8,128)(2,1)S(1)} async-done(((bf16[4,96,1024]{2,1,0:T(8,128)(2,1)}), bf16[4,96,1024]{2,1,0:T(8,128)(2,1)S(1)}, u32[]{:S(2)}, u32[]{:S(2)}) %all-to-all-start) | async-done | bytes 786464 | tf_op jit(solution)/shard_map/all_to_all | solution.py:27
  35.2 1.2 gather_fusion
  36.4 0.2 reshape.224
  36.6 0.4 copy.30
  37.0 0.3 reshape_reshape.3
  37.3 0.9 copy.20
  38.2 3.5 %all-to-all-start.2 = ((bf16[64,4,8,128]{3,2,0,1:T(8,128)(2,1)}), bf16[64,4,8,128]{3,2,0,1:T(8,128)(2,1)S(1)}, u32[]{:S(2)}, u32[]{:S(2)}) async-start(bf16[64,4,8,128]{3,2,0,1:T(8,128)(2,1)} %copy.20), calls=%async_computation.2 | async-start | bytes 1048576 | tf_op jit(solution)/shard_map/all_to_all | solution.py:65
  41.6 0.0 reduce-scatter.2.cloned.1.call-start
  41.7 0.0 collective-permute-done
  41.7 0.0 copy-done.1
  41.7 0.1 maximum_select_fusion.2
  41.8 2.0 %collective-permute-start.1 = (bf16[128,1024]{1,0:T(8,128)(2,1)S(1)}, bf16[128,1024]{1,0:T(8,128)(2,1)S(1)}, u32[]{:S(2)}, u32[]{:S(2)}) collective-permute-start(bf16[128,1024]{1,0:T(8,128)(2,1)S(1)} %maximum_select_fusion.2), channel_id=1, source_target_pairs={{0,2},{1,3},{2,0},{3,1},{4,6},{5,7},{6,4},{7,5},{8,10},{9,11},{10,... | collective-permute-start | bytes 786440 | tf_op jit(solution)/shard_map/ppermute | solution.py:70
  43.8 9.6 %collective-permute-done.1 = bf16[128,1024]{1,0:T(8,128)(2,1)S(1)} collective-permute-done((bf16[128,1024]{1,0:T(8,128)(2,1)S(1)}, bf16[128,1024]{1,0:T(8,128)(2,1)S(1)}, u32[]{:S(2)}, u32[]{:S(2)}) %collective-permute-start.1) | collective-permute-done | bytes 262176 | tf_op jit(solution)/shard_map/ppermute | solution.py:70
  53.3 0.0 all-to-all-done.2
  53.3 2.7 %fusion.2 = f32[1024,1024]{1,0:T(8,128)} fusion(bf16[32,8,8,128]{3,2,1,0:T(8,128)(2,1)S(1)} %bitcast.67, bf16[128,1024]{1,0:T(8,128)(2,1)S(1)} %collective-permute-done.1, bf16[128,1024]{1,0:T(8,128)(2,1)S(1)} %maximum_select_fusion.2, pred[]{:T(512)S(6)} %eq.49), kind=kOutput, calls=%fused_computation.9 | convolution fusion | flops 539230208 | bytes 5242881 | tf_op jit(solution)/shard_map/dot_general | solution.py:75
  56.0 0.0 copy-start.2
  56.0 0.0 reduce-scatter.2.cloned.1.call-update
  56.1 6.0 %convolution_convert_fusion = bf16[64,4096]{1,0:T(8,128)(2,1)S(1)} fusion(bf16[4096,1024]{1,0:T(8,128)(2,1)} %param.7, bf16[1,64,1024]{2,1,0:T(8,128)(2,1)S(1)} %copy-done.1), kind=kOutput, calls=%fused_computation.5 | convolution fusion | flops 537133056 | bytes 9043968 | tf_op jit(solution)/shard_map/dot_general | solution.py:48
  62.1 0.4 reshape.226
  62.5 0.4 copy.29
  62.9 0.2 reshape.267
  63.1 2.6 %scatter_custom_fusion.2 = bf16[384,1024]{1,0:T(8,128)(2,1)} fusion(s32[256]{0:T(256)S(1)} %compare_select_fusion.6, bf16[256,1024]{1,0:T(8,128)(2,1)S(1)} %reshape.267, bf16[]{:T(256)} %constant.15.clone.1), kind=kCustom, calls=%fused_computation.23 | custom fusion | bytes 786434 | tf_op jit(solution)/shard_map/scatter | solution.py:56
  65.7 3.5 %all-to-all-start.1 = ((bf16[4,96,1024]{2,1,0:T(8,128)(2,1)}), bf16[4,96,1024]{2,1,0:T(8,128)(2,1)S(1)}, u32[]{:S(2)}, u32[]{:S(2)}) async-start(bf16[4,96,1024]{2,1,0:T(8,128)(2,1)} %bitcast.14), calls=%async_computation.1 | async-start | bytes 1572864 | tf_op jit(solution)/shard_map/all_to_all | solution.py:57
  69.2 0.0 copy-done.2
  69.2 45.0 %psum.7 = f32[1024]{0:T(1024)S(1)} all-reduce(f32[1024]{0:T(1024)S(1)} %convert_reduce_fusion), channel_id=1, replica_groups=mesh['view'=8,'span'=4] {'view','span'}, use_global_device_ids=true, to_apply=%region_8.9 | all-reduce | flops 1024 | bytes 8192 | tf_op jit(solution)/shard_map/psum | solution.py:79
  114.2 0.6 broadcast_multiply_fusion.1
  114.8 0.4 reshape.225
  115.2 0.0 all-to-all-done.1
  115.2 2.0 %gather_fusion.1 = bf16[256,1024]{1,0:T(8,128)(2,1)} fusion(bf16[384,1024]{1,0:T(8,128)(2,1)S(1)} %bitcast.64, s32[1024]{0:T(1024)S(1)} %pad_clamp_fusion), kind=kCustom, calls=%fused_computation.1 | custom fusion | bytes 1049600 | tf_op jit(solution)/shard_map/gather | solution.py:60
  117.2 5.6 %fusion.1 = bf16[1,64,1024]{2,1,0:T(8,128)(2,1)} fusion(bf16[64,4096]{1,0:T(8,128)(2,1)S(1)} %reshape.225, bf16[4096,1024]{1,0:T(8,128)(2,1)} %param.7, f32[1024]{0:T(1024)S(1)} %convert_element_type.18), kind=kOutput, calls=%fused_computation.8 | convolution fusion | flops 537001984 | bytes 9048064 | tf_op jit(solution)/shard_map/dot_general | solution.py:45
  122.8 1.9 %broadcast_multiply_fusion = f32[128,1024]{1,0:T(8,128)} fusion(f32[128,1024]{1,0:T(8,128)} %reduce-scatter.2.cloned.1.call-done), kind=kLoop, calls=%fused_computation.28 | loop fusion | flops 131072 | bytes 1048576 | tf_op jit(solution)/shard_map/mul | solution.py:81
  (16 shorter events, 0.2 us)
Async XLA Ops:
  7.2 8.1 %copy-start = (bf16[1,256,1024]{2,1,0:T(8,128)(2,1)S(1)}, bf16[1,256,1024]{2,1,0:T(8,128)(2,1)}, u32[]{:S(2)}) copy-start(bf16[1,256,1024]{2,1,0:T(8,128)(2,1)} %param.5) | copy-start | bytes 1572868
  7.2 34.5 %copy-start.1 = (bf16[1,64,1024]{2,1,0:T(8,128)(2,1)S(1)}, bf16[1,64,1024]{2,1,0:T(8,128)(2,1)}, u32[]{:S(2)}) copy-start(bf16[1,64,1024]{2,1,0:T(8,128)(2,1)} %param.9) | copy-start | bytes 393220
  17.8 17.4 %all-to-all-start = ((bf16[4,96,1024]{2,1,0:T(8,128)(2,1)}), bf16[4,96,1024]{2,1,0:T(8,128)(2,1)S(1)}, u32[]{:S(2)}, u32[]{:S(2)}) async-start(bf16[4,96,1024]{2,1,0:T(8,128)(2,1)} %bitcast.6), calls=%async_computation | async-start | bytes 1572864 | tf_op jit(solution)/shard_map/all_to_all | solution.py:27
  23.0 18.7 %collective-permute-start = (bf16[64,1024]{1,0:T(8,128)(2,1)}, bf16[64,1024]{1,0:T(8,128)(2,1)S(1)}, u32[]{:S(2)}, u32[]{:S(2)}) collective-permute-start(bf16[64,1024]{1,0:T(8,128)(2,1)} %bitcast.70), channel_id=1, source_target_pairs={{0,1},{1,0},{2,3},{3,2},{4,5},{5,4},{6,7},{7,6},{8,9},{9,8},{10,11... | collective-permute-start | bytes 393224 | tf_op jit(solution)/shard_map/ppermute | solution.py:70
  38.2 15.2 %all-to-all-start.2 = ((bf16[64,4,8,128]{3,2,0,1:T(8,128)(2,1)}), bf16[64,4,8,128]{3,2,0,1:T(8,128)(2,1)S(1)}, u32[]{:S(2)}, u32[]{:S(2)}) async-start(bf16[64,4,8,128]{3,2,0,1:T(8,128)(2,1)} %copy.20), calls=%async_computation.2 | async-start | bytes 1048576 | tf_op jit(solution)/shard_map/all_to_all | solution.py:65
  41.6 81.2 %reduce-scatter.2.cloned.1.call-start = ((), (), s32[]{:S(2)}) async-start(), calls=%async_computation.4 | async-start | bytes 4718592 | tf_op jit(solution)/shard_map/reduce_scatter | solution.py:78
  41.8 11.6 %collective-permute-start.1 = (bf16[128,1024]{1,0:T(8,128)(2,1)S(1)}, bf16[128,1024]{1,0:T(8,128)(2,1)S(1)}, u32[]{:S(2)}, u32[]{:S(2)}) collective-permute-start(bf16[128,1024]{1,0:T(8,128)(2,1)S(1)} %maximum_select_fusion.2), channel_id=1, source_target_pairs={{0,2},{1,3},{2,0},{3,1},{4,6},{5,7},{6,4},{7,5},{8,10},{9,11},{10,... | collective-permute-start | bytes 786440 | tf_op jit(solution)/shard_map/ppermute | solution.py:70
  56.0 13.1 %copy-start.2 = (bf16[1024]{0:T(1024)(128)(2,1)S(1)}, bf16[1024]{0:T(1024)(128)(2,1)}, u32[]{:S(2)}) copy-start(bf16[1024]{0:T(1024)(128)(2,1)} %param.8) | copy-start | bytes 6148
  65.7 49.6 %all-to-all-start.1 = ((bf16[4,96,1024]{2,1,0:T(8,128)(2,1)}), bf16[4,96,1024]{2,1,0:T(8,128)(2,1)S(1)}, u32[]{:S(2)}, u32[]{:S(2)}) async-start(bf16[4,96,1024]{2,1,0:T(8,128)(2,1)} %bitcast.14), calls=%async_computation.1 | async-start | bytes 1572864 | tf_op jit(solution)/shard_map/all_to_all | solution.py:57
Sparse Core Ops, SparseCore 0:
  56.2 51.2 reduce-scatter.1
